TPU v7x, 32 devices: a whole 2x2x4 slice. The times are simulated.
32 devices in a mesh: dp: 8 (over z, x), mp: 4 (over y, core).
Axes of the slice: x: 2, y: 2, z: 4, core: 2. Of those that a mesh axis runs over, the one named last changes fastest.
Arguments:
- tokens: bfloat16 [2, 16384, 768], P(None, ('dp', 'mp')), may hold values from -6 to 6
- norm_gains: bfloat16 [768, 2], P('dp'), may hold values from 0.5 to 1.5
- norm_biases: bfloat16 [768, 2], P('dp'), may hold values from -3 to 3
- w_query: bfloat16 [768, 768], P('dp', 'mp'), may hold values from -0.21875 to 0.21875
- w_keyval: bfloat16 [768, 128], P('dp'), may hold values from -0.21875 to 0.21875
- w_output: bfloat16 [768, 768], P('dp', 'mp'), may hold values from -1.5 to 1.5
- w_up: bfloat16 [768, 3072], P('dp', 'mp'), may hold values from -0.21875 to 0.21875
- w_down: bfloat16 [768, 3072], P('dp', 'mp'), may hold values from -0.109375 to 0.109375
- cotangent: bfloat16 [2, 16384, 768], P(None, ('dp', 'mp')), may hold values from -6 to 6
- subset_ids: int32 [32768], P('dp'), may hold values from 0 to 21
- subset_weights: float32 [22], replicated, may hold values from 0.25 to 4
Outputs:
- output: bfloat16 [2, 16384, 768], P(None, ('dp', 'mp'))
- kv_cache: bfloat16 [32768, 128], P('dp')
- input_grad: bfloat16 [2, 16384, 768], P(None, ('dp', 'mp'))
- grad_gains: float32 [768, 2], P('dp')
- grad_biases: float32 [768, 2], P('dp')
- grad_query: float32 [768, 768], P('dp', 'mp')
- grad_keyval: float32 [768, 128], P('dp')
- grad_output: float32 [768, 768], P('dp', 'mp')
- grad_up: float32 [768, 3072], P('dp', 'mp')
- grad_down: float32 [768, 3072], P('dp', 'mp')
All inputs are finite; a program needn't handle non-finite values.
Results may differ from a plain program's by a relative error of at most 0.012.
Values may be sent and summed in bfloat16 or wider, within the bound.
A program may use at most 256 MiB of HBM per device.

v0:
```python
import jax
import jax.numpy as jnp
from jax import lax
from jax.sharding import PartitionSpec as P

HD = 64
ROT = 16
SEQ_LEN = 2048
QB = 512
epsilon = 1e-05
sqrt_half = 0.7071067811865476
inv_sqrt_two_pi = 0.3989422804014327


def rotary_tables():
    position = jnp.arange(SEQ_LEN, dtype=jnp.float32)
    frequency = 10000.0 ** (-2.0 * jnp.arange(ROT // 2, dtype=jnp.float32) / ROT)
    angles = position[:, None] * frequency[None, :]
    return (jnp.cos(angles), jnp.sin(angles))


def rotate(vectors, cosine, sine_table):
    first_half = vectors[..., : ROT // 2]
    second_half = vectors[..., ROT // 2 : ROT]
    cos_wide = cosine[:, None, :]
    sin_wide = sine_table[:, None, :]
    return jnp.concatenate(
        [
            first_half * cos_wide - second_half * sin_wide,
            second_half * cos_wide + first_half * sin_wide,
            vectors[..., ROT:],
        ],
        axis=-1,
    )


def causal_scores(query_block, key_rows, row_begin, finish):
    scores = jnp.einsum(
        "sqhd,skd->shqk", query_block, key_rows[:, :finish], preferred_element_type=jnp.float32
    )
    row_ids = row_begin + jnp.arange(QB, dtype=jnp.int32)
    col_ids = jnp.arange(finish, dtype=jnp.int32)
    causal = col_ids[None, :] <= row_ids[:, None]
    return jnp.where(causal, scores, -1e30)


def attention_forward(queries, key_rows, value_rows):
    blocks = SEQ_LEN // QB
    pieces = []
    log_norms = []
    for block_index in range(blocks):
        row_begin = block_index * QB
        finish = row_begin + QB
        scores = causal_scores(queries[:, row_begin:finish], key_rows, row_begin, finish)
        maximum = jnp.max(scores, axis=-1, keepdims=True)
        shifted = jnp.exp(scores - maximum)
        totals = jnp.sum(shifted, axis=-1, keepdims=True)
        probability = (shifted / totals).astype(jnp.bfloat16)
        pieces.append(
            jnp.einsum(
                "shqk,skd->sqhd",
                probability,
                value_rows[:, :finish],
                preferred_element_type=jnp.float32,
            )
        )
        log_norms.append(maximum + jnp.log(totals))
    return (jnp.concatenate(pieces, axis=1), log_norms)


def attention_backward(queries, key_rows, value_rows, log_norms, grad_heads):
    blocks = SEQ_LEN // QB
    length = key_rows.shape[1]
    query_pieces = []
    grad_keys = jnp.zeros(key_rows.shape, jnp.float32)
    grad_values = jnp.zeros(value_rows.shape, jnp.float32)
    for block_index in range(blocks):
        row_begin = block_index * QB
        finish = row_begin + QB
        query_block = queries[:, row_begin:finish]
        grad_block = grad_heads[:, row_begin:finish]
        scores = causal_scores(query_block, key_rows, row_begin, finish)
        probability = jnp.exp(scores - log_norms[block_index])
        grad_probs = jnp.einsum(
            "sqhd,skd->shqk", grad_block, value_rows[:, :finish], preferred_element_type=jnp.float32
        )
        inner_sum = jnp.sum(probability * grad_probs, axis=-1, keepdims=True)
        grad_scores = (probability * (grad_probs - inner_sum)).astype(jnp.bfloat16)
        query_pieces.append(
            jnp.einsum(
                "shqk,skd->sqhd",
                grad_scores,
                key_rows[:, :finish],
                preferred_element_type=jnp.float32,
            )
        )
        key_part = jnp.einsum(
            "shqk,sqhd->skd", grad_scores, query_block, preferred_element_type=jnp.float32
        )
        value_part = jnp.einsum(
            "shqk,sqhd->skd",
            probability.astype(jnp.bfloat16),
            grad_block,
            preferred_element_type=jnp.float32,
        )
        padding = ((0, 0), (0, length - finish), (0, 0))
        grad_keys = grad_keys + jnp.pad(key_part, padding)
        grad_values = grad_values + jnp.pad(value_part, padding)
    return (jnp.concatenate(query_pieces, axis=1), grad_keys, grad_values)


def shards(
    tokens,
    norm_gains,
    norm_biases,
    w_query,
    w_keyval,
    w_output,
    w_up,
    w_down,
    cotangent,
    subset_ids,
    subset_weights,
):
    micro_count = tokens.shape[0]
    own_rows = tokens.shape[1]
    micro_rows = subset_ids.shape[0] // micro_count
    sequences = micro_rows // SEQ_LEN
    head_count = w_query.shape[1] // HD
    kv_share = 1.0 / lax.axis_size("mp")
    own_begin = lax.axis_index("mp") * own_rows
    cosine, sine_table = rotary_tables()
    matches = subset_ids[:, None] == jnp.arange(subset_weights.shape[0], dtype=jnp.int32)[None, :]
    row_scale = jnp.sum(jnp.where(matches, subset_weights[None, :], 0.0), axis=1)
    outputs = []
    caches = []
    input_grads = []
    summed = None
    for micro_index in range(micro_count):
        row_begin = micro_index * micro_rows
        rows_in = tokens[micro_index]
        cot_rows = cotangent[micro_index]
        scale_rows = row_scale[row_begin : row_begin + micro_rows]
        own_scale = lax.dynamic_slice_in_dim(scale_rows, own_begin, own_rows, 0)
        gathered = (
            lax.all_gather(norm_gains, "dp", axis=0, tiled=True),
            lax.all_gather(norm_biases, "dp", axis=0, tiled=True),
            lax.all_gather(w_query, "dp", axis=0, tiled=True),
            lax.all_gather(w_keyval, "dp", axis=0, tiled=True),
            lax.all_gather(w_output, "dp", axis=0, tiled=True),
            lax.all_gather(w_up, "dp", axis=0, tiled=True),
            lax.all_gather(w_down, "dp", axis=0, tiled=True),
        )
        gains_full, biases_full, query_w, keyval_w, output_w, up_w, down_w = gathered
        rows_full = lax.all_gather(rows_in, "mp", axis=0, tiled=True).astype(jnp.float32)
        mean_row = jnp.mean(rows_full, axis=1, keepdims=True)
        centered = rows_full - mean_row
        inverse = lax.rsqrt(jnp.mean(centered * centered, axis=1, keepdims=True) + epsilon)
        normed = centered * inverse
        gains_float = gains_full.astype(jnp.float32)
        biases_float = biases_full.astype(jnp.float32)
        attn_in = (normed * gains_float[:, 0] + biases_float[:, 0]).astype(jnp.bfloat16)
        mlp_in = (normed * gains_float[:, 1] + biases_float[:, 1]).astype(jnp.bfloat16)
        query_pre = jnp.dot(attn_in, query_w, preferred_element_type=jnp.float32)
        keyval_pre = jnp.dot(attn_in, keyval_w, preferred_element_type=jnp.float32)
        queries = (
            rotate(query_pre.reshape(sequences, SEQ_LEN, head_count, HD), cosine, sine_table)
            * HD ** (-0.5)
        ).astype(jnp.bfloat16)
        key_rows = (
            rotate(keyval_pre[:, :HD].reshape(sequences, SEQ_LEN, 1, HD), cosine, sine_table)
            .astype(jnp.bfloat16)
            .reshape(sequences, SEQ_LEN, HD)
        )
        value_rows = keyval_pre[:, HD:].astype(jnp.bfloat16).reshape(sequences, SEQ_LEN, HD)
        caches.append(jnp.concatenate([key_rows, value_rows], axis=-1).reshape(micro_rows, 2 * HD))
        mixed_heads, log_norms = attention_forward(queries, key_rows, value_rows)
        heads_out = mixed_heads.reshape(micro_rows, head_count * HD).astype(jnp.bfloat16)
        hidden_pre = jnp.dot(mlp_in, up_w, preferred_element_type=jnp.float32)
        hidden = jax.nn.gelu(hidden_pre, approximate=False).astype(jnp.bfloat16)
        branch_sum = jnp.einsum(
            "rc,dc->rd", heads_out, output_w, preferred_element_type=jnp.float32
        ) + jnp.einsum("rf,df->rd", hidden, down_w, preferred_element_type=jnp.float32)
        reduced_out = lax.psum_scatter(branch_sum, "mp", scatter_dimension=0, tiled=True)
        outputs.append((reduced_out + rows_in.astype(jnp.float32)).astype(jnp.bfloat16))
        gathered_back = (
            lax.all_gather(norm_gains, "dp", axis=0, tiled=True),
            lax.all_gather(w_query, "dp", axis=0, tiled=True),
            lax.all_gather(w_keyval, "dp", axis=0, tiled=True),
            lax.all_gather(w_output, "dp", axis=0, tiled=True),
            lax.all_gather(w_up, "dp", axis=0, tiled=True),
            lax.all_gather(w_down, "dp", axis=0, tiled=True),
        )
        gains_back, query_back, keyval_back, output_back, up_back, down_back = gathered_back
        cot_full = lax.all_gather(cot_rows, "mp", axis=0, tiled=True).astype(jnp.float32)
        grad_low = (cot_full * scale_rows[:, None]).astype(jnp.bfloat16)
        grad_hidden = jnp.dot(grad_low, down_back, preferred_element_type=jnp.float32)
        normal_cdf = 0.5 * (1.0 + jax.scipy.special.erf(hidden_pre * sqrt_half))
        density = jnp.exp(-0.5 * hidden_pre * hidden_pre) * inv_sqrt_two_pi
        grad_hidden_pre = (grad_hidden * (normal_cdf + hidden_pre * density)).astype(jnp.bfloat16)
        grad_down = jnp.einsum("rd,rf->df", grad_low, hidden, preferred_element_type=jnp.float32)
        grad_up = jnp.einsum(
            "rd,rf->df", mlp_in, grad_hidden_pre, preferred_element_type=jnp.float32
        )
        grad_mlp_in = jnp.einsum(
            "rf,df->rd", grad_hidden_pre, up_back, preferred_element_type=jnp.float32
        )
        grad_heads = jnp.dot(grad_low, output_back, preferred_element_type=jnp.float32).astype(
            jnp.bfloat16
        )
        grad_output = jnp.einsum(
            "rd,rc->dc", grad_low, heads_out, preferred_element_type=jnp.float32
        )
        grad_queries, grad_keys, grad_values = attention_backward(
            queries,
            key_rows,
            value_rows,
            log_norms,
            grad_heads.reshape(sequences, SEQ_LEN, head_count, HD),
        )
        grad_query_pre = (
            (rotate(grad_queries, cosine, -sine_table) * HD ** (-0.5))
            .astype(jnp.bfloat16)
            .reshape(micro_rows, head_count * HD)
        )
        grad_query = jnp.einsum(
            "rd,rc->dc", attn_in, grad_query_pre, preferred_element_type=jnp.float32
        )
        grad_attn_query = jnp.einsum(
            "rc,dc->rd", grad_query_pre, query_back, preferred_element_type=jnp.float32
        )
        gain_part = jnp.stack(
            [jnp.sum(grad_attn_query * normed, axis=0), jnp.sum(grad_mlp_in * normed, axis=0)],
            axis=1,
        )
        bias_part = jnp.stack(
            [jnp.sum(grad_attn_query, axis=0), jnp.sum(grad_mlp_in, axis=0)], axis=1
        )
        keyval_part = jnp.concatenate([grad_keys, grad_values], axis=-1).reshape(micro_rows, 2 * HD)
        keyval_sum, gain_sum, bias_sum = lax.psum((keyval_part, gain_part, bias_part), "mp")
        grad_key_pre = rotate(
            keyval_sum[:, :HD].reshape(sequences, SEQ_LEN, 1, HD), cosine, -sine_table
        ).reshape(micro_rows, HD)
        grad_keyval_pre = jnp.concatenate([grad_key_pre, keyval_sum[:, HD:]], axis=1).astype(
            jnp.bfloat16
        )
        grad_keyval = jnp.einsum(
            "rd,rc->dc", attn_in, grad_keyval_pre, preferred_element_type=jnp.float32
        )
        grad_attn_keyval = jnp.einsum(
            "rc,dc->rd", grad_keyval_pre, keyval_back, preferred_element_type=jnp.float32
        )
        kv_gain = jnp.sum(grad_attn_keyval * normed, axis=0)
        kv_bias = jnp.sum(grad_attn_keyval, axis=0)
        grad_gains = gain_sum + jnp.stack([kv_gain, jnp.zeros_like(kv_gain)], axis=1)
        grad_biases = bias_sum + jnp.stack([kv_bias, jnp.zeros_like(kv_bias)], axis=1)
        grad_attn_in = grad_attn_query + kv_share * grad_attn_keyval
        gains_back_float = gains_back.astype(jnp.float32)
        grad_normed = grad_attn_in * gains_back_float[:, 0] + grad_mlp_in * gains_back_float[:, 1]
        centered_grad = (
            grad_normed
            - jnp.mean(grad_normed, axis=1, keepdims=True)
            - normed * jnp.mean(grad_normed * normed, axis=1, keepdims=True)
        )
        reduced_grad = lax.psum_scatter(
            centered_grad * inverse, "mp", scatter_dimension=0, tiled=True
        )
        local_rows = cot_rows.astype(jnp.float32) * own_scale[:, None]
        input_grads.append((reduced_grad + local_rows).astype(jnp.bfloat16))
        local_grads = (
            grad_gains,
            grad_biases,
            grad_query,
            grad_keyval,
            grad_output,
            grad_up,
            grad_down,
        )
        reduced = (
            lax.psum_scatter(local_grads[0], "dp", scatter_dimension=0, tiled=True),
            lax.psum_scatter(local_grads[1], "dp", scatter_dimension=0, tiled=True),
            lax.psum_scatter(local_grads[2], "dp", scatter_dimension=0, tiled=True),
            lax.psum_scatter(local_grads[3], "dp", scatter_dimension=0, tiled=True),
            lax.psum_scatter(local_grads[4], "dp", scatter_dimension=0, tiled=True),
            lax.psum_scatter(local_grads[5], "dp", scatter_dimension=0, tiled=True),
            lax.psum_scatter(local_grads[6], "dp", scatter_dimension=0, tiled=True),
        )
        summed = (
            reduced
            if summed is None
            else tuple((running + added for running, added in zip(summed, reduced)))
        )
    return (
        jnp.stack(outputs, axis=0),
        jnp.concatenate(caches, axis=0),
        jnp.stack(input_grads, axis=0),
        summed[0],
        summed[1],
        summed[2],
        summed[3],
        summed[4],
        summed[5],
        summed[6],
    )


def solution(mesh):
    return jax.shard_map(
        shards,
        mesh=mesh,
        in_specs=(
            P(None, ("dp", "mp"), None),
            P("dp", None),
            P("dp", None),
            P("dp", "mp"),
            P("dp", None),
            P("dp", "mp"),
            P("dp", "mp"),
            P("dp", "mp"),
            P(None, ("dp", "mp"), None),
            P("dp"),
            P(),
        ),
        out_specs=(
            P(None, ("dp", "mp"), None),
            P("dp", None),
            P(None, ("dp", "mp"), None),
            P("dp", None),
            P("dp", None),
            P("dp", "mp"),
            P("dp", None),
            P("dp", "mp"),
            P("dp", "mp"),
            P("dp", "mp"),
        ),
        check_vma=False,
    )
```

profile of v0, /device:TPU:0, one launch (start us, length us, event | category | flops | bytes accessed | tf_op | source)
XLA Modules:
  0.0 1251.4 jit_solution(10996470224705625093)
XLA Ops:
  15.4 22.3 %all-gather.4 = bf16[8,96,2]{1,2,0:T(2,128)(2,1)S(1)} all-gather(bf16[1,96,2]{1,2,0:T(2,128)(2,1)S(1)} %bitcast.1078), channel_id=1, replica_groups=mesh['dp'=8,'mp'=4] {'dp'}, dimensions={0}, use_global_device_ids=true | all-gather | bytes 3456 | tf_op jit(solution)/shard_map/all_gather | solution.py:146
  38.4 16.3 %all-gather.5 = bf16[8,96,2]{1,2,0:T(2,128)(2,1)S(1)} all-gather(bf16[1,96,2]{1,2,0:T(2,128)(2,1)S(1)} %bitcast.1079), channel_id=1, replica_groups=mesh['dp'=8,'mp'=4] {'dp'}, dimensions={0}, use_global_device_ids=true | all-gather | bytes 3456 | tf_op jit(solution)/shard_map/all_gather | solution.py:147
  55.5 32.6 %all_gather.25 = bf16[768,128]{1,0:T(8,128)(2,1)} all-gather(bf16[96,128]{1,0:T(8,128)(2,1)S(1)} %copy-done.158), channel_id=1, replica_groups=mesh['dp'=8,'mp'=4] {'dp'}, dimensions={0}, use_global_device_ids=true | all-gather | bytes 221184 | tf_op jit(solution)/shard_map/all_gather | solution.py:149
  89.1 33.2 %all_gather.26 = bf16[768,192]{1,0:T(8,128)(2,1)} all-gather(bf16[96,192]{1,0:T(8,128)(2,1)S(1)} %copy-done.148), channel_id=1, replica_groups=mesh['dp'=8,'mp'=4] {'dp'}, dimensions={0}, use_global_device_ids=true | all-gather | bytes 331776 | tf_op jit(solution)/shard_map/all_gather | solution.py:148
  122.3 33.3 %all_gather.27 = bf16[768,192]{1,0:T(8,128)(2,1)} all-gather(bf16[96,192]{1,0:T(8,128)(2,1)S(1)} %copy-done.149), channel_id=1, replica_groups=mesh['dp'=8,'mp'=4] {'dp'}, dimensions={0}, use_global_device_ids=true | all-gather | bytes 331776 | tf_op jit(solution)/shard_map/all_gather | solution.py:150
  281.6 11.7 fusion.126
  293.3 11.3 fusion.127
  335.5 15.2 %fusion.3 = (f32[3,512]{1,0:T(4,128)}, f32[3,512]{1,0:T(4,128)}, f32[2048,512,3]{1,0,2:T(8,128)}) fusion(f32[2048,512,3]{1,0,2:T(8,128)} %copy-done.2, f32[3,512]{1,0:T(4,128)S(1)} %log_add_fusion.4, pred[512,2048]{0,1:T(8,128)(4,1)S(1)} %copy-done.7, f32[2048,512,3]{1,0,2:T(8,128)S(1)} %fusion.296, bf16[1,2048,3,64]{1,3,2,0:T(8,128)(2,1)} %bitcast.1072, ...), kind=kOutput, calls=%fused_computation.9 | convolution fusion | flops 421524480 | bytes 39274496 | tf_op jit(solution)/shard_map/sqhd,skd->shqk/dot_general | solution.py:84
  355.6 18.4 %fusion.84 = (bf16[3,512,2048]{1,2,0:T(8,128)(2,1)S(1)}, f32[3,512]{1,0:T(4,128)S(1)}) fusion(f32[2048,512,3]{1,0,2:T(8,128)} %get-tuple-element.174, f32[2048,512,3]{1,0,2:T(8,128)} %copy-done.2, f32[3,512]{1,0:T(4,128)} %get-tuple-element.76, f32[3,512]{1,0:T(4,128)} %copy-done.133, pred[512,2048]{0,1:T(8,128)(4,1)} %iota_compare_fusion, ...), kind=kLoop, calls=%fused_computation.116 | loop fusion | flops 28310016 | bytes 57696256 | tf_op jit(solution)/shard_map/reshape.130
  374.1 12.5 fusion.85
  426.2 19.3 %fusion.68 = (bf16[2048,768]{1,0:T(8,128)(2,1)}, f32[2048,768]{1,0:T(8,128)}) fusion(bf16[768,768]{1,0:T(8,128)(2,1)} %all-gather.13.cloned.1.call-done, bf16[1,2048,768]{2,1,0:T(8,128)(2,1)} %all-gather.17.cloned.1.call-done, f32[768]{0:T(1024)S(1)} %copy-done.172, f32[768]{0:T(1024)S(1)} %copy-done.168, f32[2048]{0:T(1024)S(1)} %copy-done.144, ...), kind=kOutput, calls=%fused_computation.100 | convolution fusion | flops 2527592448 | bytes 13785088 | tf_op jit(solution)/shard_map/dot_general | solution.py:179
  445.6 17.8 %fusion.71 = (bf16[2048,768]{1,0:T(8,128)(2,1)}, f32[2048,768]{1,0:T(8,128)}) fusion(bf16[768,768]{1,0:T(8,128)(2,1)S(1)} %copy-done.180, bf16[1,2048,768]{2,1,0:T(8,128)(2,1)S(1)} %copy-done.16, f32[2048]{0:T(1024)S(1)} %copy-done.140, f32[2048]{0:T(1024)S(1)} %copy-done.127, f32[768]{0:T(1024)S(1)} %copy-done.172, f32[768]{0:T(1024)S(1)} %copy-done.168), kind=kOutput, calls=%fused_computation.103 | convolution fusion | flops 2527592448 | bytes 13785088 | tf_op jit(solution)/shard_map/dot_general | solution.py:179
  500.0 11.5 fusion.357
  519.2 10.3 all-reduce.16
  624.8 31.7 %reduce-scatter.36.cloned.1.call-done = f32[96,2]{1,0:T(8,128)} async-done(((f32[768,2]{1,0:T(8,128)}), f32[96,2]{1,0:T(8,128)}) %reduce-scatter.36.cloned.1.call-update) | async-done | bytes 784
  658.0 58.9 %reduce-scatter.16.cloned.1.call-done = f32[512,768]{1,0:T(8,128)} async-done(((f32[2048,768]{1,0:T(8,128)}), f32[512,768]{1,0:T(8,128)}) %reduce-scatter.16.cloned.1.call-update) | async-done | bytes 1572880 | tf_op jit(solution)/shard_map/reduce_scatter | solution.py:184
  716.8 61.4 %reduce-scatter.18.cloned.1.call-done = f32[512,768]{1,0:T(8,128)} async-done(((f32[2048,768]{1,0:T(8,128)}), f32[512,768]{1,0:T(8,128)}) %reduce-scatter.18.cloned.1.call-update) | async-done | bytes 1572880 | tf_op jit(solution)/shard_map/reduce_scatter | solution.py:184
  781.8 57.8 %reduce-scatter.22.cloned.1.call-done = f32[512,768]{1,0:T(8,128)} async-done(((f32[2048,768]{1,0:T(8,128)}), f32[512,768]{1,0:T(8,128)}) %reduce-scatter.22.cloned.1.call-update) | async-done | bytes 1572880 | tf_op jit(solution)/shard_map/reduce_scatter | solution.py:265
  839.6 61.4 %reduce-scatter.20.cloned.1.call-done = f32[512,768]{1,0:T(8,128)} async-done(((f32[2048,768]{1,0:T(8,128)}), f32[512,768]{1,0:T(8,128)}) %reduce-scatter.20.cloned.1.call-update) | async-done | bytes 1572880 | tf_op jit(solution)/shard_map/reduce_scatter | solution.py:265
  904.6 63.4 %reduce-scatter.28.cloned.1.call-done = f32[96,192]{1,0:T(8,128)} async-done(((f32[768,192]{1,0:T(8,128)}), f32[96,192]{1,0:T(8,128)}) %reduce-scatter.28.cloned.1.call-update) | async-done | bytes 73744 | tf_op jit(solution)/shard_map/reduce_scatter | solution.py:284
  968.0 66.1 %reduce-scatter.24.cloned.1.call-done = f32[96,192]{1,0:T(8,128)} async-done(((f32[768,192]{1,0:T(8,128)}), f32[96,192]{1,0:T(8,128)}) %reduce-scatter.24.cloned.1.call-update) | async-done | bytes 73744 | tf_op jit(solution)/shard_map/reduce_scatter | solution.py:282
  1034.1 65.0 %reduce-scatter.26.cloned.1.call-done = f32[96,128]{1,0:T(8,128)} async-done(((f32[768,128]{1,0:T(8,128)}), f32[96,128]{1,0:T(8,128)}) %reduce-scatter.26.cloned.1.call-update) | async-done | bytes 49168 | tf_op jit(solution)/shard_map/reduce_scatter | solution.py:283
  1099.1 72.5 %reduce-scatter.32.cloned.1.call-done = f32[96,768]{1,0:T(8,128)} async-done(((f32[768,768]{1,0:T(8,128)}), f32[96,768]{1,0:T(8,128)}) %reduce-scatter.32.cloned.1.call-update) | async-done | bytes 294928 | tf_op jit(solution)/shard_map/reduce_scatter | solution.py:286
  1171.6 72.7 %reduce-scatter.30.cloned.1.call-done = f32[96,768]{1,0:T(8,128)} async-done(((f32[768,768]{1,0:T(8,128)}), f32[96,768]{1,0:T(8,128)}) %reduce-scatter.30.cloned.1.call-update) | async-done | bytes 294928 | tf_op jit(solution)/shard_map/reduce_scatter | solution.py:285
  (669 shorter events, 357.2 us)
Async XLA Ops:
  7.2 152.8 %all-gather.19.cloned.1.call-start = ((), (), s32[]{:S(2)}) async-start(), calls=%async_computation.18 | async-start | bytes 3932160 | tf_op jit(solution)/shard_map/all_gather | solution.py:155
  9.9 155.6 %all-gather.17.cloned.1.call-start = ((), (), s32[]{:S(2)}) async-start(), calls=%async_computation.17 | async-start | bytes 3932160 | tf_op jit(solution)/shard_map/all_gather | solution.py:155
  10.7 178.5 %all-gather.21.cloned.1.call-start = ((), (), s32[]{:S(2)}) async-start(), calls=%async_computation.19 | async-start | bytes 3932160 | tf_op jit(solution)/shard_map/all_gather | solution.py:195
  13.4 188.3 %all-gather.23.cloned.1.call-start = ((), (), s32[]{:S(2)}) async-start(), calls=%async_computation.20 | async-start | bytes 3932160 | tf_op jit(solution)/shard_map/all_gather | solution.py:195
  14.0 412.1 %all-gather.13.cloned.1.call-start = ((), (), s32[]{:S(2)}) async-start(), calls=%async_computation.11 | async-start | bytes 1327104 | tf_op jit(solution)/shard_map/all_gather | solution.py:151
  14.6 448.8 %all-gather.15.cloned.1.call-start = ((), (), s32[]{:S(2)}) async-start(), calls=%async_computation.12 | async-start | bytes 1327104 | tf_op jit(solution)/shard_map/all_gather | solution.py:152
  15.2 479.8 %all-reduce.20.cloned.1.call-start = ((), (), s32[]{:S(2)}) async-start(), calls=%async_computation.28 | async-start | bytes 4194304 | tf_op jit(solution)/shard_map/psum | solution.py:240
  15.2 144.8 %copy-start.165 = (f32[8]{0:T(128)}, f32[8]{0:T(128)S(1)}, u32[]{:S(2)}) copy-start(f32[8]{0:T(128)S(1)} %multiply_power_fusion) | copy-start | bytes 100
  15.4 195.1 %copy-start.28 = (pred[512,512]{0,1:T(8,128)(4,1)}, pred[512,512]{0,1:T(8,128)(4,1)S(1)}, u32[]{:S(2)}) copy-start(pred[512,512]{0,1:T(8,128)(4,1)S(1)} %iota_compare_fusion.4) | copy-start | bytes 786436
  55.5 133.8 %copy-start.162 = (f32[2048]{0:T(1024)}, f32[2048]{0:T(1024)S(1)}, u32[]{:S(2)}) copy-start(f32[2048]{0:T(1024)S(1)} %get-tuple-element.152) | copy-start | bytes 24580
  55.5 146.3 %copy-start.114 = (f32[2048]{0:T(1024)}, f32[2048]{0:T(1024)S(1)}, u32[]{:S(2)}) copy-start(f32[2048]{0:T(1024)S(1)} %get-tuple-element.151) | copy-start | bytes 24580
  426.0 197.3 %reduce-scatter.34.cloned.1.call-start = ((), (), s32[]{:S(2)}) async-start(), calls=%async_computation.26 | async-start | bytes 442368
  530.4 126.1 %reduce-scatter.36.cloned.1.call-start = ((), (), s32[]{:S(2)}) async-start(), calls=%async_computation.27 | async-start | bytes 442368
  531.4 185.4 %reduce-scatter.16.cloned.1.call-start = ((), (), s32[]{:S(2)}) async-start(), calls=%async_computation.13 | async-start | bytes 7864320 | tf_op jit(solution)/shard_map/reduce_scatter | solution.py:184
  538.0 240.3 %reduce-scatter.18.cloned.1.call-start = ((), (), s32[]{:S(2)}) async-start(), calls=%async_computation.14 | async-start | bytes 7864320 | tf_op jit(solution)/shard_map/reduce_scatter | solution.py:184
  561.0 278.6 %reduce-scatter.22.cloned.1.call-start = ((), (), s32[]{:S(2)}) async-start(), calls=%async_computation.16 | async-start | bytes 7864320 | tf_op jit(solution)/shard_map/reduce_scatter | solution.py:265
  568.3 332.7 %reduce-scatter.20.cloned.1.call-start = ((), (), s32[]{:S(2)}) async-start(), calls=%async_computation.15 | async-start | bytes 7864320 | tf_op jit(solution)/shard_map/reduce_scatter | solution.py:265
  574.7 393.3 %reduce-scatter.28.cloned.1.call-start = ((), (), s32[]{:S(2)}) async-start(), calls=%async_computation.23 | async-start | bytes 884736 | tf_op jit(solution)/shard_map/reduce_scatter | solution.py:284
  581.5 452.6 %reduce-scatter.24.cloned.1.call-start = ((), (), s32[]{:S(2)}) async-start(), calls=%async_computation.21 | async-start | bytes 884736 | tf_op jit(solution)/shard_map/reduce_scatter | solution.py:282
  588.9 510.1 %reduce-scatter.26.cloned.1.call-start = ((), (), s32[]{:S(2)}) async-start(), calls=%async_computation.22 | async-start | bytes 442368 | tf_op jit(solution)/shard_map/reduce_scatter | solution.py:283
  595.7 575.9 %reduce-scatter.32.cloned.1.call-start = ((), (), s32[]{:S(2)}) async-start(), calls=%async_computation.25 | async-start | bytes 2654208 | tf_op jit(solution)/shard_map/reduce_scatter | solution.py:286
  605.9 638.4 %reduce-scatter.30.cloned.1.call-start = ((), (), s32[]{:S(2)}) async-start(), calls=%async_computation.24 | async-start | bytes 2654208 | tf_op jit(solution)/shard_map/reduce_scatter | solution.py:285
  616.9 161.4 %copy-start.40 = (bf16[2,512,768]{2,1,0:T(8,128)(2,1)S(1)}, bf16[2,512,768]{2,1,0:T(8,128)(2,1)}, u32[]{:S(2)}) copy-start(bf16[2,512,768]{2,1,0:T(8,128)(2,1)} %param.11) | copy-start | bytes 4718596
  621.0 280.0 %copy-start.41 = (bf16[2,512,768]{2,1,0:T(8,128)(2,1)S(1)}, bf16[2,512,768]{2,1,0:T(8,128)(2,1)}, u32[]{:S(2)}) copy-start(bf16[2,512,768]{2,1,0:T(8,128)(2,1)} %param.19) | copy-start | bytes 4718596
  (206 other events, 1885.1 us)
Sparse Core Ops, SparseCore 0:
  10.2 31.2 all-gather.18
  43.6 28.4 all-gather.16
  73.7 28.4 all-gather.20
  103.7 28.4 all-gather.22
  134.2 40.9 all-gather.12
  177.3 39.8 all-gather.14
  426.2 50.6 all-reduce.19
  530.5 61.4 reduce-scatter.33
  595.3 61.2 reduce-scatter.35
  658.9 57.8 reduce-scatter.15
  719.4 58.8 reduce-scatter.17
  780.7 58.8 reduce-scatter.21
  842.1 58.8 reduce-scatter.19
  904.8 63.1 reduce-scatter.27
  971.7 62.2 reduce-scatter.23
  1037.7 61.2 reduce-scatter.25
  1103.0 68.5 reduce-scatter.31
  1175.5 68.7 reduce-scatter.29
where the time goes:
time: 1260 us; the launch traced here: 1250 us
  waiting for transfers between devices  614 us (49%)
  matrix products  304 us (24%)
  blocking collectives  148 us (12%)
  other arithmetic  135 us (11%)
  local copies, waits for them, and re-layouts  32.3 us (3%)
  between operations  17.6 us (1%)
    reduce_scatter x2, waiting for transfers between devices, shards(): lax.psum_scatter(branch_sum, 'mp', scatter_dimension=0, tiled=True)  120 us
    reduce_scatter x2, waiting for transfers between devices, shards(): lax.psum_scatter(centered_grad * inverse, 'mp', scatter_dimension=0, tile...  119 us
    reduce_scatter x1, waiting for transfers between devices, shards(): lax.psum_scatter(local_grads[5], 'dp', scatter_dimension=0, tiled=True)  72.7 us
    reduce_scatter x1, waiting for transfers between devices, shards(): lax.psum_scatter(local_grads[6], 'dp', scatter_dimension=0, tiled=True)  72.5 us
    another operation x12, other arithmetic  66.7 us
    reduce_scatter x1, waiting for transfers between devices, shards(): lax.psum_scatter(local_grads[2], 'dp', scatter_dimension=0, tiled=True)  66.1 us
    reduce_scatter x1, waiting for transfers between devices, shards(): lax.psum_scatter(local_grads[3], 'dp', scatter_dimension=0, tiled=True)  65 us
    reduce_scatter x1, waiting for transfers between devices, shards(): lax.psum_scatter(local_grads[4], 'dp', scatter_dimension=0, tiled=True)  63.4 us
  transfers between devices with their start and end apart: 18, of which 10 were waited for; matrix products, arithmetic and copies ran while one was open for 35% of the time, Pallas kernels for 0%

commit v1 on v0

--- a/solution.py
+++ b/solution.py
@@ -142,10 +142,37 @@
         cot_rows = cotangent[micro_index]
         scale_rows = row_scale[row_begin : row_begin + micro_rows]
         own_scale = lax.dynamic_slice_in_dim(scale_rows, own_begin, own_rows, 0)
+
+        def core_apply(content):
+            p_next = lax.axis_size("dp")
+            val2 = lax.axis_index("dp")
+            r1, t_next, finding = (p_next, val2, content.shape[0])
+            block_list = [ii * r1 if k == 0 else ii for k, ii in enumerate(content.shape)]
+            local_next = lax.dynamic_update_slice_in_dim(
+                jnp.zeros(block_list, content.dtype), content, t_next * finding, axis=0
+            )
+            low = block_out = content
+            for q in range(1, r1 // 2 + 1):
+                low = lax.ppermute(
+                    low, axis_name="dp", perm=list(map(lambda k: (k, (k + 1) % r1), range(r1)))
+                )
+                local_next = lax.dynamic_update_slice_in_dim(
+                    local_next, low, (t_next - q) % r1 * finding, axis=0
+                )
+                if 2 * q < r1:
+                    heard = range(r1)
+                    known = map(lambda k: (k, (k - 1) % r1), heard)
+                    front = list(known)
+                    block_out = lax.ppermute(block_out, axis_name="dp", perm=front)
+                    local_next = lax.dynamic_update_slice_in_dim(
+                        local_next, block_out, (t_next + q) % r1 * finding, axis=0
+                    )
+            return local_next
+
         gathered = (
             lax.all_gather(norm_gains, "dp", axis=0, tiled=True),
             lax.all_gather(norm_biases, "dp", axis=0, tiled=True),
-            lax.all_gather(w_query, "dp", axis=0, tiled=True),
+            core_apply(w_query),
             lax.all_gather(w_keyval, "dp", axis=0, tiled=True),
             lax.all_gather(w_output, "dp", axis=0, tiled=True),
             lax.all_gather(w_up, "dp", axis=0, tiled=True),

time: 1260 us -> 1290 us (1.024)
  starting transfers between devices: 1.12 us -> 16.7 us
    ppermute x0 -> x7, starting transfers between devices: none -> 15.6 us  [the longest x3 12.5 us: core_apply(): block_out = lax.ppermute(block_out, axis_name='dp', perm=front)]
  transfers between devices with their start and end apart: 18 -> 25, of which waited for: 10 -> 13; matrix products, arithmetic and copies ran while one was open for 35% -> 35% of each run, Pallas kernels for 0% -> 0%
where the time goes in v1:
time: 1290 us; the launch traced here: 1280 us
  waiting for transfers between devices  623 us (48%)
  matrix products  309 us (24%)
  blocking collectives  144 us (11%)
  other arithmetic  139 us (11%)
  local copies, waits for them, and re-layouts  32.3 us (3%)
  between operations  17.6 us (1%)
  starting transfers between devices  16.7 us (1%)
    reduce_scatter x2, waiting for transfers between devices, shards(): lax.psum_scatter(branch_sum, 'mp', scatter_dimension=0, tiled=True)  120 us
    reduce_scatter x2, waiting for transfers between devices, shards(): lax.psum_scatter(centered_grad * inverse, 'mp', scatter_dimension=0, tile...  119 us
    reduce_scatter x1, waiting for transfers between devices, shards(): lax.psum_scatter(local_grads[5], 'dp', scatter_dimension=0, tiled=True)  72.7 us
    reduce_scatter x1, waiting for transfers between devices, shards(): lax.psum_scatter(local_grads[6], 'dp', scatter_dimension=0, tiled=True)  72.5 us
    another operation x12, other arithmetic  70.2 us
    reduce_scatter x1, waiting for transfers between devices, shards(): lax.psum_scatter(local_grads[2], 'dp', scatter_dimension=0, tiled=True)  66 us
    reduce_scatter x1, waiting for transfers between devices, shards(): lax.psum_scatter(local_grads[3], 'dp', scatter_dimension=0, tiled=True)  65 us
    reduce_scatter x1, waiting for transfers between devices, shards(): lax.psum_scatter(local_grads[4], 'dp', scatter_dimension=0, tiled=True)  63.4 us
  transfers between devices with their start and end apart: 25, of which 13 were waited for; matrix products, arithmetic and copies ran while one was open for 35% of the time, Pallas kernels for 0%

profile of v1, /device:TPU:0, one launch (start us, length us, event | category | flops | bytes accessed | tf_op | source)
XLA Modules:
  0.0 1281.6 jit_solution(5229562784572510491)
XLA Ops:
  21.0 33.0 %all_gather.59 = bf16[768,192]{1,0:T(8,128)(2,1)} all-gather(bf16[96,192]{1,0:T(8,128)(2,1)S(1)} %copy-done.121), channel_id=1, replica_groups=mesh['dp'=8,'mp'=4] {'dp'}, dimensions={0}, use_global_device_ids=true | all-gather | bytes 331776 | tf_op jit(solution)/shard_map/all_gather | solution.py:215
  54.0 18.3 %all-gather.4 = bf16[8,96,2]{1,2,0:T(2,128)(2,1)S(1)} all-gather(bf16[1,96,2]{1,2,0:T(2,128)(2,1)S(1)} %bitcast.1078), channel_id=1, replica_groups=mesh['dp'=8,'mp'=4] {'dp'}, dimensions={0}, use_global_device_ids=true | all-gather | bytes 3456 | tf_op jit(solution)/shard_map/all_gather | solution.py:173
  73.0 16.3 %all-gather.5 = bf16[8,96,2]{1,2,0:T(2,128)(2,1)S(1)} all-gather(bf16[1,96,2]{1,2,0:T(2,128)(2,1)S(1)} %bitcast.1079), channel_id=1, replica_groups=mesh['dp'=8,'mp'=4] {'dp'}, dimensions={0}, use_global_device_ids=true | all-gather | bytes 3456 | tf_op jit(solution)/shard_map/all_gather | solution.py:174
  91.7 33.0 %all_gather.26 = bf16[768,192]{1,0:T(8,128)(2,1)} all-gather(bf16[96,192]{1,0:T(8,128)(2,1)S(1)} %copy-done.143), channel_id=1, replica_groups=mesh['dp'=8,'mp'=4] {'dp'}, dimensions={0}, use_global_device_ids=true | all-gather | bytes 331776 | tf_op jit(solution)/shard_map/all_gather | solution.py:177
  129.2 32.9 %all_gather.25 = bf16[768,128]{1,0:T(8,128)(2,1)} all-gather(bf16[96,128]{1,0:T(8,128)(2,1)S(1)} %copy-done.152), channel_id=1, replica_groups=mesh['dp'=8,'mp'=4] {'dp'}, dimensions={0}, use_global_device_ids=true | all-gather | bytes 221184 | tf_op jit(solution)/shard_map/all_gather | solution.py:176
  307.7 11.7 fusion.126
  319.4 11.3 fusion.127
  360.9 15.2 %fusion.3 = (f32[3,512]{1,0:T(4,128)}, f32[3,512]{1,0:T(4,128)}, f32[2048,512,3]{1,0,2:T(8,128)}) fusion(f32[2048,512,3]{1,0,2:T(8,128)} %copy-done.2, f32[3,512]{1,0:T(4,128)S(1)} %log_add_fusion.4, pred[512,2048]{0,1:T(8,128)(4,1)S(1)} %copy-done.7, f32[2048,512,3]{1,0,2:T(8,128)S(1)} %fusion.296, bf16[1,2048,3,64]{1,3,2,0:T(8,128)(2,1)} %bitcast.1072, ...), kind=kOutput, calls=%fused_computation.9 | convolution fusion | flops 421524480 | bytes 39274496 | tf_op jit(solution)/shard_map/sqhd,skd->shqk/dot_general | solution.py:84
  381.0 18.4 %fusion.84 = (bf16[3,512,2048]{1,2,0:T(8,128)(2,1)S(1)}, f32[3,512]{1,0:T(4,128)S(1)}) fusion(f32[2048,512,3]{1,0,2:T(8,128)} %get-tuple-element.174, f32[2048,512,3]{1,0,2:T(8,128)} %copy-done.2, f32[3,512]{1,0:T(4,128)} %get-tuple-element.76, f32[3,512]{1,0:T(4,128)} %copy-done.129, pred[512,2048]{0,1:T(8,128)(4,1)} %iota_compare_fusion, ...), kind=kLoop, calls=%fused_computation.116 | loop fusion | flops 28310016 | bytes 57696256 | tf_op jit(solution)/shard_map/reshape.130
  399.5 16.0 %fusion.85 = bf16[3,512,2048]{1,2,0:T(8,128)(2,1)} fusion(f32[2048,512,3]{1,0,2:T(8,128)} %fusion.281, f32[2048,512,3]{1,0,2:T(8,128)} %copy-done, f32[3,512]{1,0:T(4,128)S(1)} %get-tuple-element.129, f32[3,512]{1,0:T(4,128)S(1)} %log_add_fusion, pred[512,2048]{0,1:T(8,128)(4,1)S(1)} %copy-done.8), kind=kLoop, calls=%fused_computation.117 | loop fusion | flops 15728640 | bytes 32518144 | tf_op jit(solution)/shard_map/reshape.188
  458.1 19.7 %fusion.68 = (bf16[2048,768]{1,0:T(8,128)(2,1)}, f32[2048,768]{1,0:T(8,128)}) fusion(bf16[768,768]{1,0:T(8,128)(2,1)} %all-gather.13.cloned.1.call-done, bf16[1,2048,768]{2,1,0:T(8,128)(2,1)} %all-gather.17.cloned.1.call-done, f32[768]{0:T(1024)} %get-tuple-element.87, f32[768]{0:T(1024)} %get-tuple-element.85, f32[2048]{0:T(1024)} %copy-done.139, ...), kind=kOutput, calls=%fused_computation.100 | convolution fusion | flops 2527592448 | bytes 13785088 | tf_op jit(solution)/shard_map/dot_general | solution.py:206
  477.8 17.9 %fusion.71 = (bf16[2048,768]{1,0:T(8,128)(2,1)}, f32[2048,768]{1,0:T(8,128)}) fusion(bf16[768,768]{1,0:T(8,128)(2,1)S(1)} %copy-done.174, bf16[1,2048,768]{2,1,0:T(8,128)(2,1)S(1)} %copy-done.15, f32[2048]{0:T(1024)S(1)} %copy-done.136, f32[2048]{0:T(1024)S(1)} %copy-done.123, f32[768]{0:T(1024)S(1)} %copy-done.166, f32[768]{0:T(1024)S(1)} %copy-done.162), kind=kOutput, calls=%fused_computation.103 | convolution fusion | flops 2527592448 | bytes 13785088 | tf_op jit(solution)/shard_map/dot_general | solution.py:206
  532.3 11.5 fusion.357
  551.4 10.3 all-reduce.16
  657.2 29.8 %reduce-scatter.36.cloned.1.call-done = f32[96,2]{1,0:T(8,128)} async-done(((f32[768,2]{1,0:T(8,128)}), f32[96,2]{1,0:T(8,128)}) %reduce-scatter.36.cloned.1.call-update) | async-done | bytes 784
  688.4 58.9 %reduce-scatter.16.cloned.1.call-done = f32[512,768]{1,0:T(8,128)} async-done(((f32[2048,768]{1,0:T(8,128)}), f32[512,768]{1,0:T(8,128)}) %reduce-scatter.16.cloned.1.call-update) | async-done | bytes 1572880 | tf_op jit(solution)/shard_map/reduce_scatter | solution.py:211
  747.3 61.4 %reduce-scatter.18.cloned.1.call-done = f32[512,768]{1,0:T(8,128)} async-done(((f32[2048,768]{1,0:T(8,128)}), f32[512,768]{1,0:T(8,128)}) %reduce-scatter.18.cloned.1.call-update) | async-done | bytes 1572880 | tf_op jit(solution)/shard_map/reduce_scatter | solution.py:211
  812.2 57.8 %reduce-scatter.22.cloned.1.call-done = f32[512,768]{1,0:T(8,128)} async-done(((f32[2048,768]{1,0:T(8,128)}), f32[512,768]{1,0:T(8,128)}) %reduce-scatter.22.cloned.1.call-update) | async-done | bytes 1572880 | tf_op jit(solution)/shard_map/reduce_scatter | solution.py:292
  869.9 61.4 %reduce-scatter.20.cloned.1.call-done = f32[512,768]{1,0:T(8,128)} async-done(((f32[2048,768]{1,0:T(8,128)}), f32[512,768]{1,0:T(8,128)}) %reduce-scatter.20.cloned.1.call-update) | async-done | bytes 1572880 | tf_op jit(solution)/shard_map/reduce_scatter | solution.py:292
  935.0 63.4 %reduce-scatter.28.cloned.1.call-done = f32[96,192]{1,0:T(8,128)} async-done(((f32[768,192]{1,0:T(8,128)}), f32[96,192]{1,0:T(8,128)}) %reduce-scatter.28.cloned.1.call-update) | async-done | bytes 73744 | tf_op jit(solution)/shard_map/reduce_scatter | solution.py:311
  998.3 66.0 %reduce-scatter.24.cloned.1.call-done = f32[96,192]{1,0:T(8,128)} async-done(((f32[768,192]{1,0:T(8,128)}), f32[96,192]{1,0:T(8,128)}) %reduce-scatter.24.cloned.1.call-update) | async-done | bytes 73744 | tf_op jit(solution)/shard_map/reduce_scatter | solution.py:309
  1064.3 65.0 %reduce-scatter.26.cloned.1.call-done = f32[96,128]{1,0:T(8,128)} async-done(((f32[768,128]{1,0:T(8,128)}), f32[96,128]{1,0:T(8,128)}) %reduce-scatter.26.cloned.1.call-update) | async-done | bytes 49168 | tf_op jit(solution)/shard_map/reduce_scatter | solution.py:310
  1129.3 72.5 %reduce-scatter.32.cloned.1.call-done = f32[96,768]{1,0:T(8,128)} async-done(((f32[768,768]{1,0:T(8,128)}), f32[96,768]{1,0:T(8,128)}) %reduce-scatter.32.cloned.1.call-update) | async-done | bytes 294928 | tf_op jit(solution)/shard_map/reduce_scatter | solution.py:313
  1201.9 72.7 %reduce-scatter.30.cloned.1.call-done = f32[96,768]{1,0:T(8,128)} async-done(((f32[768,768]{1,0:T(8,128)}), f32[96,768]{1,0:T(8,128)}) %reduce-scatter.30.cloned.1.call-update) | async-done | bytes 294928 | tf_op jit(solution)/shard_map/reduce_scatter | solution.py:312
  (680 shorter events, 389.8 us)
Async XLA Ops:
  7.2 177.3 %all-gather.19.cloned.1.call-start = ((), (), s32[]{:S(2)}) async-start(), calls=%async_computation.18 | async-start | bytes 3932160 | tf_op jit(solution)/shard_map/all_gather | solution.py:182
  9.9 180.2 %all-gather.17.cloned.1.call-start = ((), (), s32[]{:S(2)}) async-start(), calls=%async_computation.17 | async-start | bytes 3932160 | tf_op jit(solution)/shard_map/all_gather | solution.py:182
  10.7 203.1 %all-gather.21.cloned.1.call-start = ((), (), s32[]{:S(2)}) async-start(), calls=%async_computation.19 | async-start | bytes 3932160 | tf_op jit(solution)/shard_map/all_gather | solution.py:222
  13.4 212.8 %all-gather.23.cloned.1.call-start = ((), (), s32[]{:S(2)}) async-start(), calls=%async_computation.20 | async-start | bytes 3932160 | tf_op jit(solution)/shard_map/all_gather | solution.py:222
  14.0 444.0 %all-gather.13.cloned.1.call-start = ((), (), s32[]{:S(2)}) async-start(), calls=%async_computation.11 | async-start | bytes 1327104 | tf_op jit(solution)/shard_map/all_gather | solution.py:178
  14.6 481.1 %all-gather.15.cloned.1.call-start = ((), (), s32[]{:S(2)}) async-start(), calls=%async_computation.12 | async-start | bytes 1327104 | tf_op jit(solution)/shard_map/all_gather | solution.py:179
  14.7 147.4 %collective-permute-start = (bf16[96,192]{1,0:T(8,128)(2,1)S(1)}, bf16[96,192]{1,0:T(8,128)(2,1)S(1)}, u32[]{:S(2)}, u32[]{:S(2)}) collective-permute-start(bf16[96,192]{1,0:T(8,128)(2,1)S(1)} %copy-done.121), channel_id=1, source_target_pairs={{0,4},{4,8},{8,12},{12,16},{16,20},{20,24},{24,28},{28,0},{1,5},{5... | collective-permute-start | bytes 110600 | tf_op jit(solution)/shard_map/ppermute | solution.py:156
  17.7 144.5 %collective-permute-start.1 = (bf16[96,192]{1,0:T(8,128)(2,1)S(1)}, bf16[96,192]{1,0:T(8,128)(2,1)S(1)}, u32[]{:S(2)}, u32[]{:S(2)}) collective-permute-start(bf16[96,192]{1,0:T(8,128)(2,1)S(1)} %copy-done.121), channel_id=1, source_target_pairs={{0,28},{4,0},{8,4},{12,8},{16,12},{20,16},{24,20},{28,24},{1,29},{... | collective-permute-start | bytes 110600 | tf_op jit(solution)/shard_map/ppermute | solution.py:166
  20.8 506.4 %all-reduce.20.cloned.1.call-start = ((), (), s32[]{:S(2)}) async-start(), calls=%async_computation.28 | async-start | bytes 4194304 | tf_op jit(solution)/shard_map/psum | solution.py:267
  162.1 7.7 collective-permute-start.2
  162.2 7.7 collective-permute-start.3
  169.8 7.2 collective-permute-start.4
  169.8 7.2 collective-permute-start.5
  457.9 197.8 %reduce-scatter.34.cloned.1.call-start = ((), (), s32[]{:S(2)}) async-start(), calls=%async_computation.26 | async-start | bytes 442368
  562.7 124.3 %reduce-scatter.36.cloned.1.call-start = ((), (), s32[]{:S(2)}) async-start(), calls=%async_computation.27 | async-start | bytes 442368
  563.7 183.6 %reduce-scatter.16.cloned.1.call-start = ((), (), s32[]{:S(2)}) async-start(), calls=%async_computation.13 | async-start | bytes 7864320 | tf_op jit(solution)/shard_map/reduce_scatter | solution.py:211
  570.3 238.4 %reduce-scatter.18.cloned.1.call-start = ((), (), s32[]{:S(2)}) async-start(), calls=%async_computation.14 | async-start | bytes 7864320 | tf_op jit(solution)/shard_map/reduce_scatter | solution.py:211
  593.2 276.7 %reduce-scatter.22.cloned.1.call-start = ((), (), s32[]{:S(2)}) async-start(), calls=%async_computation.16 | async-start | bytes 7864320 | tf_op jit(solution)/shard_map/reduce_scatter | solution.py:292
  600.6 330.8 %reduce-scatter.20.cloned.1.call-start = ((), (), s32[]{:S(2)}) async-start(), calls=%async_computation.15 | async-start | bytes 7864320 | tf_op jit(solution)/shard_map/reduce_scatter | solution.py:292
  607.0 391.4 %reduce-scatter.28.cloned.1.call-start = ((), (), s32[]{:S(2)}) async-start(), calls=%async_computation.23 | async-start | bytes 884736 | tf_op jit(solution)/shard_map/reduce_scatter | solution.py:311
  613.7 450.6 %reduce-scatter.24.cloned.1.call-start = ((), (), s32[]{:S(2)}) async-start(), calls=%async_computation.21 | async-start | bytes 884736 | tf_op jit(solution)/shard_map/reduce_scatter | solution.py:309
  621.2 508.1 %reduce-scatter.26.cloned.1.call-start = ((), (), s32[]{:S(2)}) async-start(), calls=%async_computation.22 | async-start | bytes 442368 | tf_op jit(solution)/shard_map/reduce_scatter | solution.py:310
  628.0 573.8 %reduce-scatter.32.cloned.1.call-start = ((), (), s32[]{:S(2)}) async-start(), calls=%async_computation.25 | async-start | bytes 2654208 | tf_op jit(solution)/shard_map/reduce_scatter | solution.py:313
  638.2 636.3 %reduce-scatter.30.cloned.1.call-start = ((), (), s32[]{:S(2)}) async-start(), calls=%async_computation.24 | async-start | bytes 2654208 | tf_op jit(solution)/shard_map/reduce_scatter | solution.py:312
  (207 other events, 2992.3 us)
Sparse Core Ops, SparseCore 0:
  10.2 31.2 all-gather.18
  43.6 28.4 all-gather.16
  73.7 28.4 all-gather.20
  103.7 28.4 all-gather.22
  134.2 42.2 all-gather.12
  178.5 39.8 all-gather.14
  458.0 48.4 all-reduce.19
  562.8 59.6 reduce-scatter.33
  625.7 61.2 reduce-scatter.35
  689.3 57.8 reduce-scatter.15
  749.8 58.8 reduce-scatter.17
  811.0 58.8 reduce-scatter.21
  872.5 58.8 reduce-scatter.19
  935.1 63.1 reduce-scatter.27
  1002.0 62.2 reduce-scatter.23
  1068.0 61.2 reduce-scatter.25
  1133.2 68.5 reduce-scatter.31
  1205.8 68.6 reduce-scatter.29
